TPU v7x, 32 devices: a whole 2x2x4 slice. The times are simulated.
32 devices in a mesh: group: 4 (over y, core), member: 8 (over z, x).
Axes of the slice: x: 2, y: 2, z: 4, core: 2. Of those that a mesh axis runs over, the one named last changes fastest.
Arguments:
- features: bfloat16 [16384, 128], P(('group', 'member')), may hold values from -6 to 6
- edge_tiles: bfloat16 [8192, 128, 128], P(('group', 'member')), may hold values from -0.09375 to 0.09375
- tile_slot: int32 [32, 256], P(('group', 'member')), may hold values from 0 to 7
- tile_column: int32 [32, 256], P(('group', 'member')), may hold values from 0 to 31
- mirror_count: int32 [32, 4], P(('group', 'member')), may hold values from 0 to 2, as said below
- mirror_block: int32 [32, 4, 2], P(('group', 'member')), may hold values from 0 to 3, as said below
- weight_first: bfloat16 [128, 256], replicated, may hold values from -0.5 to 0.5
- bias_first: float32 [256], replicated, may hold values from -3 to 3
- weight_second: bfloat16 [256, 256], replicated, may hold values from -0.375 to 0.375
- bias_second: float32 [256], replicated, may hold values from -3 to 3
Outputs:
- layer_out: bfloat16 [16384, 256], P(('group', 'member'))
Inputs may be any that keep to these rules, and one draw needn't show every extreme that they name: `mirror_count`: at most 2 live mirror slots of one device for one destination group. `mirror_block`: the 2 entries of one device and destination group are distinct.
All inputs are finite; a program needn't handle non-finite values.
Results may differ from a plain program's by a relative error of at most 0.01.
Values may be sent and summed in bfloat16 or wider, within the bound.
A program may use at most 64 MiB of HBM per device.

v0:
```python
import math
import jax
import jax.numpy as jnp
from jax import lax
from jax.sharding import PartitionSpec as P


def expand(owners, block_count):
    return (owners[..., None] == jnp.arange(block_count)[None, None, :]).astype(jnp.bfloat16)


def fold_tiles(sources, edge_tiles, slot_ids, column_ids, alive_mask, slot_total):
    tile_total = edge_tiles.shape[0]
    tile_size = edge_tiles.shape[1]
    channels = sources.shape[2]
    block_tiles = math.gcd(tile_total, 32)
    rounds = tile_total // block_tiles
    tile_sets = edge_tiles.reshape(rounds, block_tiles, tile_size, tile_size)
    slot_sets = slot_ids.reshape(rounds, block_tiles)
    column_sets = column_ids.reshape(rounds, block_tiles)
    alive_sets = alive_mask.astype(jnp.float32).reshape(rounds, block_tiles)

    def advance(totals, pieces):
        tile_set, column_set, slot_set, alive_set = pieces
        source = jnp.take(sources, column_set, axis=0)
        products = jnp.einsum("tij,tjf->tif", tile_set, source, preferred_element_type=jnp.float32)
        return (totals.at[slot_set].add(products * alive_set[:, None, None]), None)

    start = jnp.zeros((slot_total, tile_size, channels), jnp.float32)
    totals, _ = lax.scan(advance, start, (tile_sets, column_sets, slot_sets, alive_sets))
    return totals.astype(jnp.bfloat16)


def body(
    features,
    edge_tiles,
    tile_slot,
    tile_column,
    mirror_count,
    mirror_block,
    weight_first,
    bias_first,
    weight_second,
    bias_second,
):
    group_count = lax.axis_size("group")
    slot_room = mirror_block.shape[2]
    tile_size = edge_tiles.shape[1]
    block_count = features.shape[0] // tile_size
    slot_ids = tile_slot[0]
    column_ids = tile_column[0]
    counts = mirror_count[0]
    targets = mirror_block[0]
    dest_group = slot_ids // slot_room
    within = slot_ids % slot_room
    count_of = jnp.sum(
        jnp.where(dest_group[:, None] == jnp.arange(group_count)[None, :], counts[None, :], 0),
        axis=1,
    )
    alive_mask = within < count_of
    spread = expand(targets, block_count)
    slot_total = group_count * slot_room

    def reduce_rows(partials):
        channels = partials.shape[2]
        spread_sums = jnp.einsum(
            "gcb,gcif->gbif",
            spread,
            partials.reshape(group_count, slot_room, tile_size, channels),
            preferred_element_type=jnp.float32,
        )
        return lax.psum_scatter(
            spread_sums.reshape(group_count * block_count, tile_size, channels).astype(
                jnp.bfloat16
            ),
            "group",
            scatter_dimension=0,
            tiled=True,
        ).astype(jnp.float32)

    local_rows = features.reshape(block_count, tile_size, features.shape[1])
    gathered = lax.all_gather(local_rows, "member", axis=0, tiled=True)
    first_sum = reduce_rows(
        fold_tiles(gathered, edge_tiles, slot_ids, column_ids, alive_mask, slot_total)
    ).astype(jnp.bfloat16)
    flat = first_sum.reshape(-1, first_sum.shape[2])
    result = jnp.maximum(
        jnp.dot(flat, weight_first, preferred_element_type=jnp.float32) + bias_first, 0.0
    )
    hidden = result.astype(jnp.bfloat16).reshape(first_sum.shape[0], tile_size, -1)
    sources = lax.all_gather(hidden, "member", axis=0, tiled=True)
    second = reduce_rows(
        fold_tiles(sources, edge_tiles, slot_ids, column_ids, alive_mask, slot_total)
    ).astype(jnp.bfloat16)
    flat_second = second.reshape(block_count * tile_size, -1)
    return (
        jnp.dot(flat_second, weight_second, preferred_element_type=jnp.float32) + bias_second
    ).astype(jnp.bfloat16)


def solution(mesh):
    placed = (
        P(("group", "member"), None),
        P(("group", "member"), None, None),
        P(("group", "member"), None),
        P(("group", "member"), None),
        P(("group", "member"), None),
        P(("group", "member"), None, None),
        P(),
        P(),
        P(),
        P(),
    )
    return jax.shard_map(
        body, mesh=mesh, in_specs=placed, out_specs=P(("group", "member"), None), check_vma=False
    )
```

profile of v0, /device:TPU:0, one launch (start us, length us, event | category | flops | bytes accessed | tf_op | source)
XLA Modules:
  0.0 324.9 jit_solution(12725843926485415464)
XLA Ops:
  13.1 39.3 %all-gather.3.cloned.1.call-done = bf16[32,128,128]{2,1,0:T(8,128)(2,1)} async-done(((bf16[4,128,128]{2,1,0:T(8,128)(2,1)}), bf16[32,128,128]{2,1,0:T(8,128)(2,1)}) %all-gather.3.cloned.1.call-update) | async-done | bytes 1048592 | tf_op jit(solution)/shard_map/all_gather | solution.py:82
  52.4 62.0 %while.20 = (s32[]{:T(128)}, f32[8,128,128]{2,1,0:T(8,128)S(1)}, s32[8,32]{1,0:T(8,128)S(1)}, bf16[8,32,128,128]{3,2,1,0:T(8,128)(2,1)}, s32[8,32]{1,0:T(8,128)S...) while((s32[]{:T(128)}, f32[8,128,128]{2,1,0:T(8,128)S(1)}, s32[8,32]{1,0:T(8,128)S(1)}, ...), condition=%wide.region_3.4_spmd, body=%wide.region_1.3_spmd.sunk | while | flops 135792000 | bytes 12589089 | solution.py:30
  52.5 2.9 gather_fusion
  60.2 2.9 gather_fusion
  67.9 2.9 gather_fusion
  75.7 2.9 gather_fusion
  83.4 2.9 gather_fusion
  88.5 2.7 scatter_fusion
  91.2 2.9 gather_fusion
  98.9 2.9 gather_fusion
  104.0 2.7 scatter_fusion
  106.7 2.9 gather_fusion
  116.0 20.5 %reduce-scatter.3.cloned.1.call-done = bf16[4,128,128]{2,1,0:T(8,128)(2,1)} async-done(((bf16[16,128,128]{2,1,0:T(8,128)(2,1)}), bf16[4,128,128]{2,1,0:T(8,128)(2,1)}) %reduce-scatter.3.cloned.1.call-update) | async-done | bytes 131088 | tf_op jit(solution)/shard_map/reduce_scatter | solution.py:72
  138.4 49.8 %all-gather.5.cloned.1.call-done = bf16[32,128,256]{2,1,0:T(8,128)(2,1)} async-done(((bf16[4,128,256]{2,1,0:T(8,128)(2,1)}), bf16[32,128,256]{2,1,0:T(8,128)(2,1)}) %all-gather.5.cloned.1.call-update) | async-done | bytes 2097168 | tf_op jit(solution)/shard_map/all_gather | solution.py:91
  188.3 102.1 %while.21 = (s32[]{:T(128)}, f32[8,128,256]{2,1,0:T(8,128)S(1)}, s32[8,32]{1,0:T(8,128)S(1)}, bf16[8,32,128,128]{3,2,1,0:T(8,128)(2,1)}, s32[8,32]{1,0:T(8,128)S...) while((s32[]{:T(128)}, f32[8,128,256]{2,1,0:T(8,128)S(1)}, s32[8,32]{1,0:T(8,128)S(1)}, ...), condition=%wide.region_7.8_spmd, body=%wide.region_5.7_spmd.sunk | while | flops 271582592 | bytes 24123424 | solution.py:30
  190.7 3.9 %convolution_multiply_fusion.5 = f32[32,128,256]{2,1,0:T(8,128)} fusion(f32[32]{0:T(128)S(1)} %fusion.53, bf16[32,128,256]{2,1,0:T(8,128)(2,1)S(1)} %gather_fusion.1, pred[32]{0:T(512)(128)(4,1)S(1)} %compare_and_fusion.5, bf16[8,32,128,128]{3,2,1,0:T(8,128)(2,1)} %get-tuple-element.250, s32[]{:T(128)} %get-tuple-element.239), kind=kOutput, calls=%fused_computation.24.clone.1 | convolution fusion | flops 270532608 | bytes 7340704 | tf_op jit(solution)/shard_map/while/body/eval_jaxpr/tij,tjf->tif/dot_general | solution.py:26
  194.6 6.4 %scatter_fusion.1 = f32[8,128,256]{2,1,0:T(8,128)S(1)} fusion(f32[8,128,256]{2,1,0:T(8,128)S(1)} %get-tuple-element.240, s32[32]{0:T(128)S(1)} %get-tuple-element.205, f32[32,128,256]{2,1,0:T(8,128)} %convolution_multiply_fusion.5), kind=kCustom, calls=%fused_computation.3.clone.1 | custom fusion | flops 1048576 | bytes 12583040 | tf_op jit(solution)/shard_map/while/body/eval_jaxpr/scatter-add | solution.py:27
  203.4 3.9 %convolution_multiply_fusion.5 = f32[32,128,256]{2,1,0:T(8,128)} fusion(f32[32]{0:T(128)S(1)} %fusion.53, bf16[32,128,256]{2,1,0:T(8,128)(2,1)S(1)} %gather_fusion.1, pred[32]{0:T(512)(128)(4,1)S(1)} %compare_and_fusion.5, bf16[8,32,128,128]{3,2,1,0:T(8,128)(2,1)} %get-tuple-element.250, s32[]{:T(128)} %get-tuple-element.239), kind=kOutput, calls=%fused_computation.24.clone.1 | convolution fusion | flops 270532608 | bytes 7340704 | tf_op jit(solution)/shard_map/while/body/eval_jaxpr/tij,tjf->tif/dot_general | solution.py:26
  207.3 6.4 %scatter_fusion.1 = f32[8,128,256]{2,1,0:T(8,128)S(1)} fusion(f32[8,128,256]{2,1,0:T(8,128)S(1)} %get-tuple-element.240, s32[32]{0:T(128)S(1)} %get-tuple-element.205, f32[32,128,256]{2,1,0:T(8,128)} %convolution_multiply_fusion.5), kind=kCustom, calls=%fused_computation.3.clone.1 | custom fusion | flops 1048576 | bytes 12583040 | tf_op jit(solution)/shard_map/while/body/eval_jaxpr/scatter-add | solution.py:27
  216.2 3.9 %convolution_multiply_fusion.5 = f32[32,128,256]{2,1,0:T(8,128)} fusion(f32[32]{0:T(128)S(1)} %fusion.53, bf16[32,128,256]{2,1,0:T(8,128)(2,1)S(1)} %gather_fusion.1, pred[32]{0:T(512)(128)(4,1)S(1)} %compare_and_fusion.5, bf16[8,32,128,128]{3,2,1,0:T(8,128)(2,1)} %get-tuple-element.250, s32[]{:T(128)} %get-tuple-element.239), kind=kOutput, calls=%fused_computation.24.clone.1 | convolution fusion | flops 270532608 | bytes 7340704 | tf_op jit(solution)/shard_map/while/body/eval_jaxpr/tij,tjf->tif/dot_general | solution.py:26
  220.1 6.5 %scatter_fusion.1 = f32[8,128,256]{2,1,0:T(8,128)S(1)} fusion(f32[8,128,256]{2,1,0:T(8,128)S(1)} %get-tuple-element.240, s32[32]{0:T(128)S(1)} %get-tuple-element.205, f32[32,128,256]{2,1,0:T(8,128)} %convolution_multiply_fusion.5), kind=kCustom, calls=%fused_computation.3.clone.1 | custom fusion | flops 1048576 | bytes 12583040 | tf_op jit(solution)/shard_map/while/body/eval_jaxpr/scatter-add | solution.py:27
  228.9 3.9 %convolution_multiply_fusion.5 = f32[32,128,256]{2,1,0:T(8,128)} fusion(f32[32]{0:T(128)S(1)} %fusion.53, bf16[32,128,256]{2,1,0:T(8,128)(2,1)S(1)} %gather_fusion.1, pred[32]{0:T(512)(128)(4,1)S(1)} %compare_and_fusion.5, bf16[8,32,128,128]{3,2,1,0:T(8,128)(2,1)} %get-tuple-element.250, s32[]{:T(128)} %get-tuple-element.239), kind=kOutput, calls=%fused_computation.24.clone.1 | convolution fusion | flops 270532608 | bytes 7340704 | tf_op jit(solution)/shard_map/while/body/eval_jaxpr/tij,tjf->tif/dot_general | solution.py:26
  232.9 6.5 %scatter_fusion.1 = f32[8,128,256]{2,1,0:T(8,128)S(1)} fusion(f32[8,128,256]{2,1,0:T(8,128)S(1)} %get-tuple-element.240, s32[32]{0:T(128)S(1)} %get-tuple-element.205, f32[32,128,256]{2,1,0:T(8,128)} %convolution_multiply_fusion.5), kind=kCustom, calls=%fused_computation.3.clone.1 | custom fusion | flops 1048576 | bytes 12583040 | tf_op jit(solution)/shard_map/while/body/eval_jaxpr/scatter-add | solution.py:27
  241.7 3.9 %convolution_multiply_fusion.5 = f32[32,128,256]{2,1,0:T(8,128)} fusion(f32[32]{0:T(128)S(1)} %fusion.53, bf16[32,128,256]{2,1,0:T(8,128)(2,1)S(1)} %gather_fusion.1, pred[32]{0:T(512)(128)(4,1)S(1)} %compare_and_fusion.5, bf16[8,32,128,128]{3,2,1,0:T(8,128)(2,1)} %get-tuple-element.250, s32[]{:T(128)} %get-tuple-element.239), kind=kOutput, calls=%fused_computation.24.clone.1 | convolution fusion | flops 270532608 | bytes 7340704 | tf_op jit(solution)/shard_map/while/body/eval_jaxpr/tij,tjf->tif/dot_general | solution.py:26
  245.6 6.4 %scatter_fusion.1 = f32[8,128,256]{2,1,0:T(8,128)S(1)} fusion(f32[8,128,256]{2,1,0:T(8,128)S(1)} %get-tuple-element.240, s32[32]{0:T(128)S(1)} %get-tuple-element.205, f32[32,128,256]{2,1,0:T(8,128)} %convolution_multiply_fusion.5), kind=kCustom, calls=%fused_computation.3.clone.1 | custom fusion | flops 1048576 | bytes 12583040 | tf_op jit(solution)/shard_map/while/body/eval_jaxpr/scatter-add | solution.py:27
  254.4 3.9 %convolution_multiply_fusion.5 = f32[32,128,256]{2,1,0:T(8,128)} fusion(f32[32]{0:T(128)S(1)} %fusion.53, bf16[32,128,256]{2,1,0:T(8,128)(2,1)S(1)} %gather_fusion.1, pred[32]{0:T(512)(128)(4,1)S(1)} %compare_and_fusion.5, bf16[8,32,128,128]{3,2,1,0:T(8,128)(2,1)} %get-tuple-element.250, s32[]{:T(128)} %get-tuple-element.239), kind=kOutput, calls=%fused_computation.24.clone.1 | convolution fusion | flops 270532608 | bytes 7340704 | tf_op jit(solution)/shard_map/while/body/eval_jaxpr/tij,tjf->tif/dot_general | solution.py:26
  258.4 6.4 %scatter_fusion.1 = f32[8,128,256]{2,1,0:T(8,128)S(1)} fusion(f32[8,128,256]{2,1,0:T(8,128)S(1)} %get-tuple-element.240, s32[32]{0:T(128)S(1)} %get-tuple-element.205, f32[32,128,256]{2,1,0:T(8,128)} %convolution_multiply_fusion.5), kind=kCustom, calls=%fused_computation.3.clone.1 | custom fusion | flops 1048576 | bytes 12583040 | tf_op jit(solution)/shard_map/while/body/eval_jaxpr/scatter-add | solution.py:27
  267.2 3.9 %convolution_multiply_fusion.5 = f32[32,128,256]{2,1,0:T(8,128)} fusion(f32[32]{0:T(128)S(1)} %fusion.53, bf16[32,128,256]{2,1,0:T(8,128)(2,1)S(1)} %gather_fusion.1, pred[32]{0:T(512)(128)(4,1)S(1)} %compare_and_fusion.5, bf16[8,32,128,128]{3,2,1,0:T(8,128)(2,1)} %get-tuple-element.250, s32[]{:T(128)} %get-tuple-element.239), kind=kOutput, calls=%fused_computation.24.clone.1 | convolution fusion | flops 270532608 | bytes 7340704 | tf_op jit(solution)/shard_map/while/body/eval_jaxpr/tij,tjf->tif/dot_general | solution.py:26
  271.1 6.5 %scatter_fusion.1 = f32[8,128,256]{2,1,0:T(8,128)S(1)} fusion(f32[8,128,256]{2,1,0:T(8,128)S(1)} %get-tuple-element.240, s32[32]{0:T(128)S(1)} %get-tuple-element.205, f32[32,128,256]{2,1,0:T(8,128)} %convolution_multiply_fusion.5), kind=kCustom, calls=%fused_computation.3.clone.1 | custom fusion | flops 1048576 | bytes 12583040 | tf_op jit(solution)/shard_map/while/body/eval_jaxpr/scatter-add | solution.py:27
  279.9 3.9 %convolution_multiply_fusion.5 = f32[32,128,256]{2,1,0:T(8,128)} fusion(f32[32]{0:T(128)S(1)} %fusion.53, bf16[32,128,256]{2,1,0:T(8,128)(2,1)S(1)} %gather_fusion.1, pred[32]{0:T(512)(128)(4,1)S(1)} %compare_and_fusion.5, bf16[8,32,128,128]{3,2,1,0:T(8,128)(2,1)} %get-tuple-element.250, s32[]{:T(128)} %get-tuple-element.239), kind=kOutput, calls=%fused_computation.24.clone.1 | convolution fusion | flops 270532608 | bytes 7340704 | tf_op jit(solution)/shard_map/while/body/eval_jaxpr/tij,tjf->tif/dot_general | solution.py:26
  283.9 6.5 %scatter_fusion.1 = f32[8,128,256]{2,1,0:T(8,128)S(1)} fusion(f32[8,128,256]{2,1,0:T(8,128)S(1)} %get-tuple-element.240, s32[32]{0:T(128)S(1)} %get-tuple-element.205, f32[32,128,256]{2,1,0:T(8,128)} %convolution_multiply_fusion.5), kind=kCustom, calls=%fused_computation.3.clone.1 | custom fusion | flops 1048576 | bytes 12583040 | tf_op jit(solution)/shard_map/while/body/eval_jaxpr/scatter-add | solution.py:27
  292.9 23.6 %reduce-scatter.5.cloned.1.call-done = bf16[4,128,256]{2,1,0:T(8,128)(2,1)} async-done(((bf16[16,128,256]{2,1,0:T(8,128)(2,1)}), bf16[4,128,256]{2,1,0:T(8,128)(2,1)}) %reduce-scatter.5.cloned.1.call-update) | async-done | bytes 262160 | tf_op jit(solution)/shard_map/reduce_scatter | solution.py:72
  (122 shorter events, 65.7 us)
Async XLA Ops:
  6.5 309.9 %copy-start = (bf16[256,256]{1,0:T(8,128)(2,1)S(1)}, bf16[256,256]{1,0:T(8,128)(2,1)}, u32[]{:S(2)}) copy-start(bf16[256,256]{1,0:T(8,128)(2,1)} %param.22) | copy-start | bytes 393220
  6.5 45.8 %all-gather.3.cloned.1.call-start = ((), (), s32[]{:S(2)}) async-start(), calls=%async_computation.2 | async-start | bytes 1179648 | tf_op jit(solution)/shard_map/all_gather | solution.py:82
  7.3 129.3 %reduce-scatter.3.cloned.1.call-start = ((), (), s32[]{:S(2)}) async-start(), calls=%async_computation.3 | async-start | bytes 655360 | tf_op jit(solution)/shard_map/reduce_scatter | solution.py:72
  114.4 22.2 %copy-start.1 = (bf16[128,256]{1,0:T(8,128)(2,1)S(1)}, bf16[128,256]{1,0:T(8,128)(2,1)}, u32[]{:S(2)}) copy-start(bf16[128,256]{1,0:T(8,128)(2,1)} %param.20) | copy-start | bytes 196612
  114.4 22.1 %copy-start.2 = (f32[256]{0:T(256)S(1)}, f32[256]{0:T(256)}, u32[]{:S(2)}) copy-start(f32[256]{0:T(256)} %param.21) | copy-start | bytes 3076
  116.0 72.2 %all-gather.5.cloned.1.call-start = ((), (), s32[]{:S(2)}) async-start(), calls=%async_computation.4 | async-start | bytes 2359296 | tf_op jit(solution)/shard_map/all_gather | solution.py:91
  138.4 178.1 %reduce-scatter.5.cloned.1.call-start = ((), (), s32[]{:S(2)}) async-start(), calls=%async_computation.5 | async-start | bytes 1310720 | tf_op jit(solution)/shard_map/reduce_scatter | solution.py:72
  291.7 24.8 %copy-start.3 = (f32[256]{0:T(256)S(1)}, f32[256]{0:T(256)}, u32[]{:S(2)}) copy-start(f32[256]{0:T(256)} %param.23) | copy-start | bytes 3076
Sparse Core Ops, SparseCore 0:
  9.5 42.8 all-gather.2
  116.1 20.4 reduce-scatter.2
  138.9 49.2 all-gather.4
  293.0 23.4 reduce-scatter.4
where the time goes:
time: 327 us; the launch traced here: 325 us
  waiting for transfers between devices  134 us (41%)
  other arithmetic  77.7 us (24%)
  matrix products  53.4 us (16%)
  local copies, waits for them, and re-layouts  45.6 us (14%)
  between operations  13.2 us (4%)
    scatter-add x16, other arithmetic, advance(): return (totals.at[slot_set].add(products * alive_set[:, None, None]), None)  72.9 us
    all_gather x1, waiting for transfers between devices, body(): sources = lax.all_gather(hidden, 'member', axis=0, tiled=True)  49.8 us
    dot_general x16, matrix products, advance(): jnp.einsum('tij,tjf->tif', tile_set, source, preferred_element_type=jnp.f...  47.9 us
    reduce_scatter x2, waiting for transfers between devices, reduce_rows(): lax.psum_scatter(spread_sums.reshape(group_count * block_count, tile_size...  44.1 us
    gather x16, local copies, waits for them, and re-layouts, advance(): source = jnp.take(sources, column_set, axis=0)  41.7 us
    all_gather x1, waiting for transfers between devices, body(): gathered = lax.all_gather(local_rows, 'member', axis=0, tiled=True)  39.3 us
  transfers between devices with their start and end apart: 4, of which 4 were waited for; matrix products, arithmetic and copies ran while one was open for 2% of the time, Pallas kernels for 0%

commit v1 on v0

--- a/solution.py
+++ b/solution.py
@@ -79,7 +79,19 @@
         ).astype(jnp.float32)
 
     local_rows = features.reshape(block_count, tile_size, features.shape[1])
-    gathered = lax.all_gather(local_rows, "member", axis=0, tiled=True)
+    world_n = lax.axis_size("member")
+    seen = [local_rows]
+    dev_j = 0
+    while dev_j < world_n - 1:
+        a_now = lax.ppermute(
+            seen[-1], axis_name="member", perm=[(it, (it + 1) % world_n) for it in range(world_n)]
+        )
+        seen.append(a_now)
+        dev_j = dev_j + 1
+    field_out = jnp.concatenate(seen[::-1], axis=0)
+    gathered = jnp.roll(
+        field_out, shift=(lax.axis_index("member") + 1) * local_rows.shape[0], axis=0
+    )
     first_sum = reduce_rows(
         fold_tiles(gathered, edge_tiles, slot_ids, column_ids, alive_mask, slot_total)
     ).astype(jnp.bfloat16)

time: 327 us -> 339 us (1.037)
  waiting for transfers between devices: 134 us -> 141 us
    ppermute x0 -> x7, waiting for transfers between devices: none -> 48.3 us  [body(): lax.ppermute(seen[-1], axis_name='member', perm=[(it, (it + 1) % world_n)...]
    all_gather x1 -> x0, waiting for transfers between devices: 39.3 us -> none  [body(): gathered = lax.all_gather(local_rows, 'member', axis=0, tiled=True)]
  transfers between devices with their start and end apart: 4 -> 10, of which waited for: 4 -> 10; matrix products, arithmetic and copies ran while one was open for 2% -> 2% of each run, Pallas kernels for 0% -> 0%
where the time goes in v1:
time: 339 us; the launch traced here: 337 us
  waiting for transfers between devices  141 us (42%)
  other arithmetic  77.5 us (23%)
  matrix products  53.5 us (16%)
  local copies, waits for them, and re-layouts  47.6 us (14%)
  between operations  13.3 us (4%)
    scatter-add x16, other arithmetic, advance(): return (totals.at[slot_set].add(products * alive_set[:, None, None]), None)  72.9 us
    all_gather x1, waiting for transfers between devices, body(): sources = lax.all_gather(hidden, 'member', axis=0, tiled=True)  49.8 us
    ppermute x7, waiting for transfers between devices, body(): lax.ppermute(seen[-1], axis_name='member', perm=[(it, (it + 1) % world_n)...  48.3 us
    dot_general x16, matrix products, advance(): jnp.einsum('tij,tjf->tif', tile_set, source, preferred_element_type=jnp.f...  48 us
    reduce_scatter x2, waiting for transfers between devices, reduce_rows(): lax.psum_scatter(spread_sums.reshape(group_count * block_count, tile_size...  42.9 us
    gather x16, local copies, waits for them, and re-layouts, advance(): source = jnp.take(sources, column_set, axis=0)  41.5 us
  transfers between devices with their start and end apart: 10, of which 10 were waited for; matrix products, arithmetic and copies ran while one was open for 2% of the time, Pallas kernels for 0%

profile of v1, /device:TPU:0, one launch (start us, length us, event | category | flops | bytes accessed | tf_op | source)
XLA Modules:
  0.0 337.0 jit_solution(12486095950152931035)
XLA Ops:
  6.5 2.9 collective-permute-start
  9.5 6.8 %collective-permute-done = bf16[4,128,128]{2,1,0:T(8,128)(2,1)S(1)} collective-permute-done((bf16[4,128,128]{2,1,0:T(8,128)(2,1)}, bf16[4,128,128]{2,1,0:T(8,128)(2,1)S(1)}, u32[]{:S(2)}, u32[]{:S(2)}) %collective-permute-start) | collective-permute-done | bytes 131104 | tf_op jit(solution)/shard_map/ppermute | solution.py:86
  16.3 7.7 %collective-permute-done.1 = bf16[4,128,128]{2,1,0:T(8,128)(2,1)S(1)} collective-permute-done((bf16[4,128,128]{2,1,0:T(8,128)(2,1)S(1)}, bf16[4,128,128]{2,1,0:T(8,128)(2,1)S(1)}, u32[]{:S(2)}, u32[]{:S(2)}) %collective-permute-start.1) | collective-permute-done | bytes 131104 | tf_op jit(solution)/shard_map/ppermute | solution.py:86
  23.9 7.7 %collective-permute-done.2 = bf16[4,128,128]{2,1,0:T(8,128)(2,1)S(1)} collective-permute-done((bf16[4,128,128]{2,1,0:T(8,128)(2,1)S(1)}, bf16[4,128,128]{2,1,0:T(8,128)(2,1)S(1)}, u32[]{:S(2)}, u32[]{:S(2)}) %collective-permute-start.2) | collective-permute-done | bytes 131104 | tf_op jit(solution)/shard_map/ppermute | solution.py:86
  31.6 7.7 %collective-permute-done.3 = bf16[4,128,128]{2,1,0:T(8,128)(2,1)S(1)} collective-permute-done((bf16[4,128,128]{2,1,0:T(8,128)(2,1)S(1)}, bf16[4,128,128]{2,1,0:T(8,128)(2,1)S(1)}, u32[]{:S(2)}, u32[]{:S(2)}) %collective-permute-start.3) | collective-permute-done | bytes 131104 | tf_op jit(solution)/shard_map/ppermute | solution.py:86
  39.3 7.7 %collective-permute-done.4 = bf16[4,128,128]{2,1,0:T(8,128)(2,1)S(1)} collective-permute-done((bf16[4,128,128]{2,1,0:T(8,128)(2,1)S(1)}, bf16[4,128,128]{2,1,0:T(8,128)(2,1)S(1)}, u32[]{:S(2)}, u32[]{:S(2)}) %collective-permute-start.4) | collective-permute-done | bytes 131104 | tf_op jit(solution)/shard_map/ppermute | solution.py:86
  52.5 3.2 collective-permute-done.5
  55.7 7.7 %collective-permute-done.6 = bf16[4,128,128]{2,1,0:T(8,128)(2,1)S(1)} collective-permute-done((bf16[4,128,128]{2,1,0:T(8,128)(2,1)S(1)}, bf16[4,128,128]{2,1,0:T(8,128)(2,1)S(1)}, u32[]{:S(2)}, u32[]{:S(2)}) %collective-permute-start.6) | collective-permute-done | bytes 131104 | tf_op jit(solution)/shard_map/ppermute | solution.py:86
  65.8 61.8 %while.20 = (s32[]{:T(128)}, f32[8,128,128]{2,1,0:T(8,128)S(1)}, s32[8,32]{1,0:T(8,128)S(1)}, bf16[8,32,128,128]{3,2,1,0:T(8,128)(2,1)}, s32[8,32]{1,0:T(8,128)S...) while((s32[]{:T(128)}, f32[8,128,128]{2,1,0:T(8,128)S(1)}, s32[8,32]{1,0:T(8,128)S(1)}, ...), condition=%wide.region_3.4_spmd, body=%wide.region_1.3_spmd.sunk | while | flops 135792000 | bytes 12589089 | solution.py:30
  65.8 2.9 gather_fusion
  73.6 2.9 gather_fusion
  81.3 2.9 gather_fusion
  129.2 19.4 %reduce-scatter.3.cloned.1.call-done = bf16[4,128,128]{2,1,0:T(8,128)(2,1)} async-done(((bf16[16,128,128]{2,1,0:T(8,128)(2,1)}), bf16[4,128,128]{2,1,0:T(8,128)(2,1)}) %reduce-scatter.3.cloned.1.call-update) | async-done | bytes 131088 | tf_op jit(solution)/shard_map/reduce_scatter | solution.py:72
  150.5 49.8 %all-gather.2.cloned.1.call-done = bf16[32,128,256]{2,1,0:T(8,128)(2,1)} async-done(((bf16[4,128,256]{2,1,0:T(8,128)(2,1)}), bf16[32,128,256]{2,1,0:T(8,128)(2,1)}) %all-gather.2.cloned.1.call-update) | async-done | bytes 2097168 | tf_op jit(solution)/shard_map/all_gather | solution.py:103
  200.4 102.2 %while.21 = (s32[]{:T(128)}, f32[8,128,256]{2,1,0:T(8,128)S(1)}, s32[8,32]{1,0:T(8,128)S(1)}, bf16[8,32,128,128]{3,2,1,0:T(8,128)(2,1)}, s32[8,32]{1,0:T(8,128)S...) while((s32[]{:T(128)}, f32[8,128,256]{2,1,0:T(8,128)S(1)}, s32[8,32]{1,0:T(8,128)S(1)}, ...), condition=%wide.region_7.8_spmd, body=%wide.region_5.7_spmd.sunk | while | flops 271582592 | bytes 24123424 | solution.py:30
  202.7 3.9 %convolution_multiply_fusion.5 = f32[32,128,256]{2,1,0:T(8,128)} fusion(f32[32]{0:T(128)S(1)} %fusion.53, bf16[32,128,256]{2,1,0:T(8,128)(2,1)S(1)} %gather_fusion.1, pred[32]{0:T(512)(128)(4,1)S(1)} %compare_and_fusion.5, bf16[8,32,128,128]{3,2,1,0:T(8,128)(2,1)} %get-tuple-element.250, s32[]{:T(128)} %get-tuple-element.239), kind=kOutput, calls=%fused_computation.24.clone.1 | convolution fusion | flops 270532608 | bytes 7340704 | tf_op jit(solution)/shard_map/while/body/eval_jaxpr/tij,tjf->tif/dot_general | solution.py:26
  206.7 6.4 %scatter_fusion.1 = f32[8,128,256]{2,1,0:T(8,128)S(1)} fusion(f32[8,128,256]{2,1,0:T(8,128)S(1)} %get-tuple-element.240, s32[32]{0:T(128)S(1)} %get-tuple-element.205, f32[32,128,256]{2,1,0:T(8,128)} %convolution_multiply_fusion.5), kind=kCustom, calls=%fused_computation.3.clone.1 | custom fusion | flops 1048576 | bytes 12583040 | tf_op jit(solution)/shard_map/while/body/eval_jaxpr/scatter-add | solution.py:27
  215.5 3.9 %convolution_multiply_fusion.5 = f32[32,128,256]{2,1,0:T(8,128)} fusion(f32[32]{0:T(128)S(1)} %fusion.53, bf16[32,128,256]{2,1,0:T(8,128)(2,1)S(1)} %gather_fusion.1, pred[32]{0:T(512)(128)(4,1)S(1)} %compare_and_fusion.5, bf16[8,32,128,128]{3,2,1,0:T(8,128)(2,1)} %get-tuple-element.250, s32[]{:T(128)} %get-tuple-element.239), kind=kOutput, calls=%fused_computation.24.clone.1 | convolution fusion | flops 270532608 | bytes 7340704 | tf_op jit(solution)/shard_map/while/body/eval_jaxpr/tij,tjf->tif/dot_general | solution.py:26
  219.4 6.4 %scatter_fusion.1 = f32[8,128,256]{2,1,0:T(8,128)S(1)} fusion(f32[8,128,256]{2,1,0:T(8,128)S(1)} %get-tuple-element.240, s32[32]{0:T(128)S(1)} %get-tuple-element.205, f32[32,128,256]{2,1,0:T(8,128)} %convolution_multiply_fusion.5), kind=kCustom, calls=%fused_computation.3.clone.1 | custom fusion | flops 1048576 | bytes 12583040 | tf_op jit(solution)/shard_map/while/body/eval_jaxpr/scatter-add | solution.py:27
  228.3 3.9 %convolution_multiply_fusion.5 = f32[32,128,256]{2,1,0:T(8,128)} fusion(f32[32]{0:T(128)S(1)} %fusion.53, bf16[32,128,256]{2,1,0:T(8,128)(2,1)S(1)} %gather_fusion.1, pred[32]{0:T(512)(128)(4,1)S(1)} %compare_and_fusion.5, bf16[8,32,128,128]{3,2,1,0:T(8,128)(2,1)} %get-tuple-element.250, s32[]{:T(128)} %get-tuple-element.239), kind=kOutput, calls=%fused_computation.24.clone.1 | convolution fusion | flops 270532608 | bytes 7340704 | tf_op jit(solution)/shard_map/while/body/eval_jaxpr/tij,tjf->tif/dot_general | solution.py:26
  232.2 6.5 %scatter_fusion.1 = f32[8,128,256]{2,1,0:T(8,128)S(1)} fusion(f32[8,128,256]{2,1,0:T(8,128)S(1)} %get-tuple-element.240, s32[32]{0:T(128)S(1)} %get-tuple-element.205, f32[32,128,256]{2,1,0:T(8,128)} %convolution_multiply_fusion.5), kind=kCustom, calls=%fused_computation.3.clone.1 | custom fusion | flops 1048576 | bytes 12583040 | tf_op jit(solution)/shard_map/while/body/eval_jaxpr/scatter-add | solution.py:27
  241.0 3.9 %convolution_multiply_fusion.5 = f32[32,128,256]{2,1,0:T(8,128)} fusion(f32[32]{0:T(128)S(1)} %fusion.53, bf16[32,128,256]{2,1,0:T(8,128)(2,1)S(1)} %gather_fusion.1, pred[32]{0:T(512)(128)(4,1)S(1)} %compare_and_fusion.5, bf16[8,32,128,128]{3,2,1,0:T(8,128)(2,1)} %get-tuple-element.250, s32[]{:T(128)} %get-tuple-element.239), kind=kOutput, calls=%fused_computation.24.clone.1 | convolution fusion | flops 270532608 | bytes 7340704 | tf_op jit(solution)/shard_map/while/body/eval_jaxpr/tij,tjf->tif/dot_general | solution.py:26
  245.0 6.5 %scatter_fusion.1 = f32[8,128,256]{2,1,0:T(8,128)S(1)} fusion(f32[8,128,256]{2,1,0:T(8,128)S(1)} %get-tuple-element.240, s32[32]{0:T(128)S(1)} %get-tuple-element.205, f32[32,128,256]{2,1,0:T(8,128)} %convolution_multiply_fusion.5), kind=kCustom, calls=%fused_computation.3.clone.1 | custom fusion | flops 1048576 | bytes 12583040 | tf_op jit(solution)/shard_map/while/body/eval_jaxpr/scatter-add | solution.py:27
  253.8 3.9 %convolution_multiply_fusion.5 = f32[32,128,256]{2,1,0:T(8,128)} fusion(f32[32]{0:T(128)S(1)} %fusion.53, bf16[32,128,256]{2,1,0:T(8,128)(2,1)S(1)} %gather_fusion.1, pred[32]{0:T(512)(128)(4,1)S(1)} %compare_and_fusion.5, bf16[8,32,128,128]{3,2,1,0:T(8,128)(2,1)} %get-tuple-element.250, s32[]{:T(128)} %get-tuple-element.239), kind=kOutput, calls=%fused_computation.24.clone.1 | convolution fusion | flops 270532608 | bytes 7340704 | tf_op jit(solution)/shard_map/while/body/eval_jaxpr/tij,tjf->tif/dot_general | solution.py:26
  257.8 6.4 %scatter_fusion.1 = f32[8,128,256]{2,1,0:T(8,128)S(1)} fusion(f32[8,128,256]{2,1,0:T(8,128)S(1)} %get-tuple-element.240, s32[32]{0:T(128)S(1)} %get-tuple-element.205, f32[32,128,256]{2,1,0:T(8,128)} %convolution_multiply_fusion.5), kind=kCustom, calls=%fused_computation.3.clone.1 | custom fusion | flops 1048576 | bytes 12583040 | tf_op jit(solution)/shard_map/while/body/eval_jaxpr/scatter-add | solution.py:27
  266.6 3.9 %convolution_multiply_fusion.5 = f32[32,128,256]{2,1,0:T(8,128)} fusion(f32[32]{0:T(128)S(1)} %fusion.53, bf16[32,128,256]{2,1,0:T(8,128)(2,1)S(1)} %gather_fusion.1, pred[32]{0:T(512)(128)(4,1)S(1)} %compare_and_fusion.5, bf16[8,32,128,128]{3,2,1,0:T(8,128)(2,1)} %get-tuple-element.250, s32[]{:T(128)} %get-tuple-element.239), kind=kOutput, calls=%fused_computation.24.clone.1 | convolution fusion | flops 270532608 | bytes 7340704 | tf_op jit(solution)/shard_map/while/body/eval_jaxpr/tij,tjf->tif/dot_general | solution.py:26
  270.5 6.4 %scatter_fusion.1 = f32[8,128,256]{2,1,0:T(8,128)S(1)} fusion(f32[8,128,256]{2,1,0:T(8,128)S(1)} %get-tuple-element.240, s32[32]{0:T(128)S(1)} %get-tuple-element.205, f32[32,128,256]{2,1,0:T(8,128)} %convolution_multiply_fusion.5), kind=kCustom, calls=%fused_computation.3.clone.1 | custom fusion | flops 1048576 | bytes 12583040 | tf_op jit(solution)/shard_map/while/body/eval_jaxpr/scatter-add | solution.py:27
  279.3 3.9 %convolution_multiply_fusion.5 = f32[32,128,256]{2,1,0:T(8,128)} fusion(f32[32]{0:T(128)S(1)} %fusion.53, bf16[32,128,256]{2,1,0:T(8,128)(2,1)S(1)} %gather_fusion.1, pred[32]{0:T(512)(128)(4,1)S(1)} %compare_and_fusion.5, bf16[8,32,128,128]{3,2,1,0:T(8,128)(2,1)} %get-tuple-element.250, s32[]{:T(128)} %get-tuple-element.239), kind=kOutput, calls=%fused_computation.24.clone.1 | convolution fusion | flops 270532608 | bytes 7340704 | tf_op jit(solution)/shard_map/while/body/eval_jaxpr/tij,tjf->tif/dot_general | solution.py:26
  283.3 6.5 %scatter_fusion.1 = f32[8,128,256]{2,1,0:T(8,128)S(1)} fusion(f32[8,128,256]{2,1,0:T(8,128)S(1)} %get-tuple-element.240, s32[32]{0:T(128)S(1)} %get-tuple-element.205, f32[32,128,256]{2,1,0:T(8,128)} %convolution_multiply_fusion.5), kind=kCustom, calls=%fused_computation.3.clone.1 | custom fusion | flops 1048576 | bytes 12583040 | tf_op jit(solution)/shard_map/while/body/eval_jaxpr/scatter-add | solution.py:27
  292.1 3.9 %convolution_multiply_fusion.5 = f32[32,128,256]{2,1,0:T(8,128)} fusion(f32[32]{0:T(128)S(1)} %fusion.53, bf16[32,128,256]{2,1,0:T(8,128)(2,1)S(1)} %gather_fusion.1, pred[32]{0:T(512)(128)(4,1)S(1)} %compare_and_fusion.5, bf16[8,32,128,128]{3,2,1,0:T(8,128)(2,1)} %get-tuple-element.250, s32[]{:T(128)} %get-tuple-element.239), kind=kOutput, calls=%fused_computation.24.clone.1 | convolution fusion | flops 270532608 | bytes 7340704 | tf_op jit(solution)/shard_map/while/body/eval_jaxpr/tij,tjf->tif/dot_general | solution.py:26
  296.1 6.5 %scatter_fusion.1 = f32[8,128,256]{2,1,0:T(8,128)S(1)} fusion(f32[8,128,256]{2,1,0:T(8,128)S(1)} %get-tuple-element.240, s32[32]{0:T(128)S(1)} %get-tuple-element.205, f32[32,128,256]{2,1,0:T(8,128)} %convolution_multiply_fusion.5), kind=kCustom, calls=%fused_computation.3.clone.1 | custom fusion | flops 1048576 | bytes 12583040 | tf_op jit(solution)/shard_map/while/body/eval_jaxpr/scatter-add | solution.py:27
  305.0 23.6 %reduce-scatter.5.cloned.1.call-done = bf16[4,128,256]{2,1,0:T(8,128)(2,1)} async-done(((bf16[16,128,256]{2,1,0:T(8,128)(2,1)}), bf16[4,128,256]{2,1,0:T(8,128)(2,1)}) %reduce-scatter.5.cloned.1.call-update) | async-done | bytes 262160 | tf_op jit(solution)/shard_map/reduce_scatter | solution.py:72
  (152 shorter events, 86.9 us)
Async XLA Ops:
  6.5 322.1 %copy-start = (bf16[256,256]{1,0:T(8,128)(2,1)S(1)}, bf16[256,256]{1,0:T(8,128)(2,1)}, u32[]{:S(2)}) copy-start(bf16[256,256]{1,0:T(8,128)(2,1)} %param.22) | copy-start | bytes 393220
  6.5 58.2 %copy-start.1 = (bf16[512,128]{1,0:T(8,128)(2,1)S(1)}, bf16[512,128]{1,0:T(8,128)(2,1)}, u32[]{:S(2)}) copy-start(bf16[512,128]{1,0:T(8,128)(2,1)} %param.14) | copy-start | bytes 393220
  6.5 142.1 %reduce-scatter.3.cloned.1.call-start = ((), (), s32[]{:S(2)}) async-start(), calls=%async_computation.2 | async-start | bytes 655360 | tf_op jit(solution)/shard_map/reduce_scatter | solution.py:72
  6.5 9.7 %collective-permute-start = (bf16[4,128,128]{2,1,0:T(8,128)(2,1)}, bf16[4,128,128]{2,1,0:T(8,128)(2,1)S(1)}, u32[]{:S(2)}, u32[]{:S(2)}) collective-permute-start(bf16[4,128,128]{2,1,0:T(8,128)(2,1)} %bitcast.86), channel_id=1, source_target_pairs={{0,1},{1,2},{2,3},{3,4},{4,5},{5,6},{6,7},{7,0},{8,9},{9,10},{10,1... | collective-permute-start | bytes 393224 | tf_op jit(solution)/shard_map/ppermute | solution.py:86
  16.3 7.7 %collective-permute-start.1 = (bf16[4,128,128]{2,1,0:T(8,128)(2,1)S(1)}, bf16[4,128,128]{2,1,0:T(8,128)(2,1)S(1)}, u32[]{:S(2)}, u32[]{:S(2)}) collective-permute-start(bf16[4,128,128]{2,1,0:T(8,128)(2,1)S(1)} %collective-permute-done), channel_id=1, source_target_pairs={{0,1},{1,2},{2,3},{3,4},{4,5},{5,6},{6,7},{7,0},{8,9},{9,10},{10,1... | collective-permute-start | bytes 393224 | tf_op jit(solution)/shard_map/ppermute | solution.py:86
  23.9 7.7 %collective-permute-start.2 = (bf16[4,128,128]{2,1,0:T(8,128)(2,1)S(1)}, bf16[4,128,128]{2,1,0:T(8,128)(2,1)S(1)}, u32[]{:S(2)}, u32[]{:S(2)}) collective-permute-start(bf16[4,128,128]{2,1,0:T(8,128)(2,1)S(1)} %collective-permute-done.1), channel_id=1, source_target_pairs={{0,1},{1,2},{2,3},{3,4},{4,5},{5,6},{6,7},{7,0},{8,9},{9,10},{10,1... | collective-permute-start | bytes 393224 | tf_op jit(solution)/shard_map/ppermute | solution.py:86
  31.6 7.7 %collective-permute-start.3 = (bf16[4,128,128]{2,1,0:T(8,128)(2,1)S(1)}, bf16[4,128,128]{2,1,0:T(8,128)(2,1)S(1)}, u32[]{:S(2)}, u32[]{:S(2)}) collective-permute-start(bf16[4,128,128]{2,1,0:T(8,128)(2,1)S(1)} %collective-permute-done.2), channel_id=1, source_target_pairs={{0,1},{1,2},{2,3},{3,4},{4,5},{5,6},{6,7},{7,0},{8,9},{9,10},{10,1... | collective-permute-start | bytes 393224 | tf_op jit(solution)/shard_map/ppermute | solution.py:86
  39.2 7.7 %collective-permute-start.4 = (bf16[4,128,128]{2,1,0:T(8,128)(2,1)S(1)}, bf16[4,128,128]{2,1,0:T(8,128)(2,1)S(1)}, u32[]{:S(2)}, u32[]{:S(2)}) collective-permute-start(bf16[4,128,128]{2,1,0:T(8,128)(2,1)S(1)} %collective-permute-done.3), channel_id=1, source_target_pairs={{0,1},{1,2},{2,3},{3,4},{4,5},{5,6},{6,7},{7,0},{8,9},{9,10},{10,1... | collective-permute-start | bytes 393224 | tf_op jit(solution)/shard_map/ppermute | solution.py:86
  46.9 8.8 %collective-permute-start.5 = (bf16[4,128,128]{2,1,0:T(8,128)(2,1)S(1)}, bf16[4,128,128]{2,1,0:T(8,128)(2,1)S(1)}, u32[]{:S(2)}, u32[]{:S(2)}) collective-permute-start(bf16[4,128,128]{2,1,0:T(8,128)(2,1)S(1)} %collective-permute-done.4), channel_id=1, source_target_pairs={{0,1},{1,2},{2,3},{3,4},{4,5},{5,6},{6,7},{7,0},{8,9},{9,10},{10,1... | collective-permute-start | bytes 393224 | tf_op jit(solution)/shard_map/ppermute | solution.py:86
  55.7 7.7 %collective-permute-start.6 = (bf16[4,128,128]{2,1,0:T(8,128)(2,1)S(1)}, bf16[4,128,128]{2,1,0:T(8,128)(2,1)S(1)}, u32[]{:S(2)}, u32[]{:S(2)}) collective-permute-start(bf16[4,128,128]{2,1,0:T(8,128)(2,1)S(1)} %collective-permute-done.5), channel_id=1, source_target_pairs={{0,1},{1,2},{2,3},{3,4},{4,5},{5,6},{6,7},{7,0},{8,9},{9,10},{10,1... | collective-permute-start | bytes 393224 | tf_op jit(solution)/shard_map/ppermute | solution.py:86
  127.6 21.0 %copy-start.2 = (bf16[128,256]{1,0:T(8,128)(2,1)S(1)}, bf16[128,256]{1,0:T(8,128)(2,1)}, u32[]{:S(2)}) copy-start(bf16[128,256]{1,0:T(8,128)(2,1)} %param.20) | copy-start | bytes 196612
  127.6 21.0 %copy-start.3 = (f32[256]{0:T(256)S(1)}, f32[256]{0:T(256)}, u32[]{:S(2)}) copy-start(f32[256]{0:T(256)} %param.21) | copy-start | bytes 3076
  129.2 71.1 %all-gather.2.cloned.1.call-start = ((), (), s32[]{:S(2)}) async-start(), calls=%async_computation.3 | async-start | bytes 2359296 | tf_op jit(solution)/shard_map/all_gather | solution.py:103
  150.4 178.2 %reduce-scatter.5.cloned.1.call-start = ((), (), s32[]{:S(2)}) async-start(), calls=%async_computation.4 | async-start | bytes 1310720 | tf_op jit(solution)/shard_map/reduce_scatter | solution.py:72
  303.8 24.8 %copy-start.4 = (f32[256]{0:T(256)S(1)}, f32[256]{0:T(256)}, u32[]{:S(2)}) copy-start(f32[256]{0:T(256)} %param.23) | copy-start | bytes 3076
Sparse Core Ops, SparseCore 0:
  129.3 19.2 reduce-scatter.2
  150.9 49.2 all-gather.1
  305.1 23.4 reduce-scatter.4
